TPU v7x, 128 devices: a whole 4x4x4 slice. The times are simulated.
128 devices in a mesh: row: 16 (over x_hi, y, core), proto: 8 (over z, x_lo).
Axes of the slice: x: 4 (x_hi: 2, x_lo: 2; x = x_hi * 2 + x_lo), y: 4, z: 4, core: 2. Of those that a mesh axis runs over, the one named last changes fastest.
Arguments:
- tokens: bfloat16 [8192, 4096], P('row'), may hold values from -6 to 6
- w_in: bfloat16 [4096, 8192], P('row', 'proto'), may hold values from -0.09375 to 0.09375
- w_out: bfloat16 [8192, 384], P('proto'), may hold values from -0.0625 to 0.0625
- teacher_z: bfloat16 [8192, 384], P(('row', 'proto')), may hold values from -6 to 6
- proto_student: bfloat16 [384, 49152], P(None, 'proto'), may hold values from -48 to 48
- proto_teacher: bfloat16 [384, 49152], P(None, 'proto'), may hold values from -48 to 48
- center: float32 [49152], P('proto'), may hold values from -0.6 to 0.6
- image_of: int32 [8192], P('row'), may hold values from 0 to 63
Outputs:
- loss: float32 [], replicated
- w_in_grad: float32 [4096, 8192], P('row', 'proto')
- w_out_grad: float32 [8192, 384], P('proto')
- proto_grad: float32 [384, 49152], P('row', 'proto')
All inputs are finite; a program needn't handle non-finite values.
Results may differ from a plain program's by a relative error of at most 0.015.
Values may be sent and summed in bfloat16 or wider, within the bound.
A program may use at most 128 MiB of HBM per device.

v0:
```python
import jax
import jax.numpy as jnp
from jax import lax
from jax.sharding import PartitionSpec as P

tau_teacher = 0.07
tau_student = 0.1
loss_scale = 1048576.0
norm_eps = 1e-06


def gelu_parts(values):
    cumul = 0.5 * (1.0 + jax.scipy.special.erf(values * 0.7071067811865476))
    density = jnp.exp(-0.5 * values * values) * 0.3989422804014327
    return (values * cumul, cumul + values * density)


def inner(left, right):
    return lax.dot_general(
        left, right, (((0,), (0,)), ((), ())), preferred_element_type=jnp.float32
    )


def outer_last(left, right):
    return lax.dot_general(
        left, right, (((1,), (1,)), ((), ())), preferred_element_type=jnp.float32
    )


def normalize(values):
    recip = lax.rsqrt(jnp.sum(values * values, axis=1, keepdims=True) + norm_eps)
    return (recip, values * recip)


def teacher_norm(teacher_z):
    teach = teacher_z.astype(jnp.float32)
    return (teach * lax.rsqrt(jnp.sum(teach * teach, axis=1, keepdims=True) + norm_eps)).astype(
        jnp.bfloat16
    )


def back_norm(dnorm, recip, unit):
    return (recip * (dnorm - unit * jnp.sum(unit * dnorm, axis=1, keepdims=True))).astype(
        jnp.bfloat16
    )


def on_device(tokens, w_in, w_out, teacher_z, proto_student, proto_teacher, center, image_of):
    row_count = tokens.shape[0]
    images = row_count * lax.axis_size("row") // 128
    onehot = (image_of[:, None] == jnp.arange(images, dtype=jnp.int32)[None, :]).astype(jnp.float32)
    counts = lax.psum(jnp.sum(onehot, axis=0), "row")
    weight = 1.0 / (images * jnp.sum(onehot * counts[None, :], axis=1))
    pre = jnp.dot(
        tokens, lax.all_gather(w_in, "row", axis=0, tiled=True), preferred_element_type=jnp.float32
    )
    act, slope = gelu_parts(pre)
    hidden = act.astype(jnp.bfloat16)
    partial_value = jnp.dot(hidden, w_out, preferred_element_type=jnp.float32)
    bott = lax.psum(partial_value, "proto")
    recip, unit = normalize(bott)
    student_n = unit.astype(jnp.bfloat16)
    teacher_n = lax.all_gather(teacher_norm(teacher_z), "proto", axis=0, tiled=True)
    logit_t = (
        jnp.dot(teacher_n, proto_teacher, preferred_element_type=jnp.float32) - center[None, :]
    ) / tau_teacher
    logit_s = jnp.dot(student_n, proto_student, preferred_element_type=jnp.float32) / tau_student
    local_t = jnp.max(logit_t, axis=1)
    local_s = jnp.max(logit_s, axis=1)
    top_t, top_s = lax.pmax((local_t, local_s), "proto")
    exp_t = jnp.exp(logit_t - top_t[:, None])
    exp_s = jnp.exp(logit_s - top_s[:, None])
    total_t, total_s = lax.psum((jnp.sum(exp_t, axis=1), jnp.sum(exp_s, axis=1)), "proto")
    prob_t = exp_t / total_t[:, None]
    prob_s = exp_s / total_s[:, None]
    logp_s = logit_s - top_s[:, None] - jnp.log(total_s)[:, None]
    cross = -jnp.sum(prob_t * logp_s, axis=1)
    loss = lax.psum(jnp.sum(weight * cross), ("row", "proto"))
    grad_s = (loss_scale * weight[:, None] * (prob_s - prob_t) / tau_student).astype(jnp.bfloat16)
    proto_grad = lax.psum_scatter(
        inner(student_n, grad_s).astype(jnp.bfloat16), "row", scatter_dimension=0, tiled=True
    ).astype(jnp.float32)
    dnorm_part = outer_last(grad_s, proto_student)
    dnorm = lax.psum(dnorm_part, "proto")
    dbott = back_norm(dnorm, recip, unit)
    w_out_grad = lax.psum(inner(hidden, dbott).astype(jnp.bfloat16), "row").astype(jnp.float32)
    dpre = (outer_last(dbott, w_out) * slope).astype(jnp.bfloat16)
    w_in_grad = lax.psum_scatter(
        inner(tokens, dpre).astype(jnp.bfloat16), "row", scatter_dimension=0, tiled=True
    ).astype(jnp.float32)
    return (loss, w_in_grad, w_out_grad, proto_grad)


def solution(mesh):
    return jax.shard_map(
        on_device,
        mesh=mesh,
        in_specs=(
            P("row", None),
            P("row", "proto"),
            P("proto", None),
            P(("row", "proto"), None),
            P(None, "proto"),
            P(None, "proto"),
            P("proto"),
            P("row"),
        ),
        out_specs=(P(), P("row", "proto"), P("proto", None), P("row", "proto")),
        check_vma=False,
    )
```

profile of v0, /device:TPU:0, one launch (start us, length us, event | category | flops | bytes accessed | tf_op | source)
XLA Modules:
  0.0 676.0 jit_solution(12270464372114535581)
XLA Ops:
  8.8 38.4 %psum.49 = f32[64]{0:T(128)S(1)} all-reduce(f32[64]{0:T(128)S(1)} %convert_reduce_fusion), channel_id=1, replica_groups=mesh['row'=16,'proto'=8] {'row'}, use_global_device_ids=true, to_apply=%region_1.0 | all-reduce | flops 64 | bytes 512 | tf_op jit(solution)/shard_map/psum | solution.py:52
  49.8 35.8 %all-gather.2.cloned.1.call-done = bf16[4096,1024]{1,0:T(8,128)(2,1)} async-done(((bf16[256,1024]{1,0:T(8,128)(2,1)}), bf16[4096,1024]{1,0:T(8,128)(2,1)}) %all-gather.2.cloned.1.call-update) | async-done | bytes 8388624 | tf_op jit(solution)/shard_map/all_gather | solution.py:55
  85.6 10.6 %multiply_convert_fusion.1 = (bf16[512,1024]{1,0:T(8,128)(2,1)S(1)}, f32[512,1024]{1,0:T(8,128)}) fusion(bf16[512,4096]{1,0:T(8,128)(2,1)} %param.8, bf16[4096,1024]{1,0:T(8,128)(2,1)} %all-gather.2.cloned.1.call-done), kind=kOutput, calls=%fused_computation.19 | convolution fusion | flops 4297588736 | bytes 15728640 | tf_op jit(solution)/shard_map/dot_general | solution.py:54
  97.8 31.3 %all_gather.6 = bf16[512,384]{1,0:T(8,128)(2,1)S(1)} all-gather(bf16[64,384]{1,0:T(8,128)(2,1)S(1)} %fusion.10), channel_id=1, replica_groups=mesh['row'=16,'proto'=8] {'proto'}, dimensions={0}, use_global_device_ids=true | all-gather | bytes 442368 | tf_op jit(solution)/shard_map/all_gather | solution.py:63
  129.1 9.0 %fusion = (f32[512]{0:T(512)S(1)}, f32[512,6144]{1,0:T(8,128)}) fusion(f32[6144]{0:T(1024)S(1)} %copy-done.3, bf16[512,384]{1,0:T(8,128)(2,1)S(1)} %all_gather.6, bf16[384,6144]{1,0:T(8,128)(2,1)} %param.13), kind=kOutput, calls=%fused_computation.7 | convolution fusion | flops 2425355776 | bytes 17721344 | tf_op jit(solution)/shard_map/dot_general | solution.py:65
  138.2 37.0 %all-reduce.6.cloned.1.call-done = f32[512,384]{1,0:T(8,128)} async-done(((f32[512,384]{1,0:T(8,128)}), f32[512,384]{1,0:T(8,128)}) %all-reduce.6.cloned.1.call-update) | async-done | bytes 786448 | tf_op jit(solution)/shard_map/psum | solution.py:60
  176.5 10.6 %multiply_reduce_fusion.1 = (f32[512]{0:T(512)S(1)}, f32[512,6144]{1,0:T(8,128)}) fusion(bf16[384,6144]{1,0:T(8,128)(2,1)} %param.12, f32[512,384]{1,0:T(8,128)} %all-reduce.6.cloned.1.call-done, f32[512]{0:T(512)S(1)} %add_rsqrt_fusion), kind=kOutput, calls=%fused_computation.6 | convolution fusion | flops 2422603264 | bytes 18092032 | tf_op jit(solution)/shard_map/dot_general | solution.py:67
  187.1 17.9 %all-reduce.1 = (f32[512]{0:T(512)S(1)}, f32[512]{0:T(512)S(1)}) all-reduce(f32[512]{0:T(512)S(1)} %get-tuple-element.20, f32[512]{0:T(512)S(1)} %get-tuple-element.22), channel_id=1, replica_groups=mesh['row'=16,'proto'=8] {'proto'}, use_global_device_ids=true, to_apply=%region_11.0 | all-reduce | flops 1024 | bytes 8192 | tf_op jit(solution)/shard_map/pmax | solution.py:70
  205.0 10.3 %exponential_reduce_fusion = (f32[512]{0:T(512)S(1)}, f32[512]{0:T(512)S(1)}) fusion(f32[512,6144]{1,0:T(8,128)} %get-tuple-element.21, f32[512]{0:T(512)S(1)} %get-tuple-element.14, f32[512]{0:T(512)S(1)} %get-tuple-element.15, f32[512,6144]{1,0:T(8,128)} %get-tuple-element.23, f32[6144]{0:T(1024)S(1)} %copy-done.3), kind=kLoop, calls=%fused_computation.4 | loop fusion | flops 22019072 | bytes 25198592 | tf_op jit(solution)/shard_map/reduce_sum | solution.py:73
  215.3 16.4 %all-reduce = (f32[512]{0:T(512)S(1)}, f32[512]{0:T(512)S(1)}) all-reduce(f32[512]{0:T(512)S(1)} %get-tuple-element.24, f32[512]{0:T(512)S(1)} %get-tuple-element.25), channel_id=1, replica_groups=mesh['row'=16,'proto'=8] {'proto'}, use_global_device_ids=true, to_apply=%region_13.0 | all-reduce | flops 1024 | bytes 8192 | tf_op jit(solution)/shard_map/psum | solution.py:73
  231.7 12.0 %multiply_convert_fusion = (bf16[512,6144]{1,0:T(8,128)(2,1)S(1)}, f32[512]{0:T(512)S(1)}) fusion(f32[512,6144]{1,0:T(8,128)} %get-tuple-element.21, f32[512]{0:T(512)S(1)} %get-tuple-element.12, f32[512]{0:T(512)S(1)} %broadcast_multiply_fusion, f32[512]{0:T(512)S(1)} %get-tuple-element.14, f32[512]{0:T(512)S(1)} %get-tuple-element.13, ...), kind=kLoop, calls=%fused_computation | loop fusion | flops 44039680 | bytes 31496192 | tf_op jit(solution)/shard_map/convert_element_type | solution.py:79
  243.7 2.7 copy-done.1
  246.3 6.7 fusion.15
  253.1 76.8 %all-reduce.8.cloned.1.call-done = f32[512,384]{1,0:T(8,128)} async-done(((f32[512,384]{1,0:T(8,128)}), f32[512,384]{1,0:T(8,128)}) %all-reduce.8.cloned.1.call-update) | async-done | bytes 786448 | tf_op jit(solution)/shard_map/psum | solution.py:84
  332.6 1.7 convolution_convert_fusion.1
  334.4 7.7 %convolution_convert_fusion = bf16[384,6144]{1,0:T(8,128)(2,1)} fusion(bf16[512,6144]{1,0:T(8,128)(2,1)} %copy-done.1, f32[512,384]{1,0:T(8,128)S(1)} %copy-done.2, f32[512]{0:T(512)S(1)} %add_rsqrt_fusion), kind=kOutput, calls=%fused_computation.10 | convolution fusion | flops 2418671616 | bytes 11798528 | tf_op jit(solution)/shard_map/dot_general | solution.py:19
  342.1 10.4 %convert_bitcast_fusion = bf16[4096,1024]{0,1:T(8,128)(2,1)} fusion(bf16[512,4096]{1,0:T(8,128)(2,1)} %param.8, f32[512,1024]{1,0:T(8,128)} %get-tuple-element.19, bf16[512,384]{1,0:T(8,128)(2,1)S(1)} %multiply_convert_fusion.2, bf16[1024,384]{1,0:T(8,128)(2,1)S(1)} %copy-done), kind=kOutput, calls=%fused_computation.11 | convolution fusion | flops 4707057664 | bytes 15859712 | tf_op jit(solution)/shard_map/dot_general | solution.py:19
  353.1 63.4 %psum.53 = f32[]{:T(128)} all-reduce(f32[]{:T(128)} %multiply_reduce_fusion.4), channel_id=1, replica_groups=mesh['row'=16,'proto'=8] {'row','proto'}, use_global_device_ids=true, to_apply=%region_16.0 | all-reduce | flops 1 | bytes 8 | tf_op jit(solution)/shard_map/psum | solution.py:78
  416.5 57.5 %all-reduce.10.cloned.1.call-done = bf16[1024,384]{1,0:T(8,128)(2,1)} async-done(((bf16[1024,384]{1,0:T(8,128)(2,1)}), bf16[1024,384]{1,0:T(8,128)(2,1)}) %all-reduce.10.cloned.1.call-update) | async-done | bytes 786448 | tf_op jit(solution)/shard_map/psum | solution.py:86
  474.0 2.4 convert_element_type.57
  476.4 85.6 %reduce-scatter.5.cloned.1.call-done = bf16[24,6144]{1,0:T(8,128)(2,1)} async-done(((bf16[384,6144]{1,0:T(8,128)(2,1)}), bf16[24,6144]{1,0:T(8,128)(2,1)}) %reduce-scatter.5.cloned.1.call-update) | async-done | bytes 294928 | tf_op jit(solution)/shard_map/reduce_scatter | solution.py:80
  561.9 1.8 convert_element_type.59
  563.7 103.1 %reduce-scatter.3.cloned.1.call-done = bf16[256,1024]{0,1:T(8,128)(2,1)} async-done(((bf16[4096,1024]{0,1:T(8,128)(2,1)}), bf16[256,1024]{0,1:T(8,128)(2,1)}) %reduce-scatter.3.cloned.1.call-update) | async-done | bytes 524304 | tf_op jit(solution)/shard_map/reduce_scatter | solution.py:88
  666.9 2.2 copy.13
  (32 shorter events, 10.6 us)
Async XLA Ops:
  7.2 89.0 %copy-start = (bf16[1024,384]{1,0:T(8,128)(2,1)S(1)}, bf16[1024,384]{1,0:T(8,128)(2,1)}, u32[]{:S(2)}) copy-start(bf16[1024,384]{1,0:T(8,128)(2,1)} %param.10) | copy-start | bytes 2359300
  7.2 78.4 %all-gather.2.cloned.1.call-start = ((), (), s32[]{:S(2)}) async-start(), calls=%async_computation.2 | async-start | bytes 8912896 | tf_op jit(solution)/shard_map/all_gather | solution.py:55
  7.9 167.3 %all-reduce.6.cloned.1.call-start = ((), (), s32[]{:S(2)}) async-start(), calls=%async_computation.3 | async-start | bytes 1572864 | tf_op jit(solution)/shard_map/psum | solution.py:60
  49.8 79.3 %copy-start.3 = (f32[6144]{0:T(1024)S(1)}, f32[6144]{0:T(1024)}, u32[]{:S(2)}) copy-start(f32[6144]{0:T(1024)} %param.14) | copy-start | bytes 73732
  97.8 232.1 %all-reduce.8.cloned.1.call-start = ((), (), s32[]{:S(2)}) async-start(), calls=%async_computation.4 | async-start | bytes 1572864 | tf_op jit(solution)/shard_map/psum | solution.py:84
  243.7 2.7 copy-start.1
  246.3 83.6 %copy-start.2 = (f32[512,384]{1,0:T(8,128)S(1)}, f32[512,384]{1,0:T(8,128)}, u32[]{:S(2)}) copy-start(f32[512,384]{1,0:T(8,128)} %all-reduce.6.cloned.1.call-done) | copy-start | bytes 2359300
  253.0 220.9 %all-reduce.10.cloned.1.call-start = ((), (), s32[]{:S(2)}) async-start(), calls=%async_computation.6 | async-start | bytes 1572864 | tf_op jit(solution)/shard_map/psum | solution.py:86
  334.3 227.6 %reduce-scatter.5.cloned.1.call-start = ((), (), s32[]{:S(2)}) async-start(), calls=%async_computation.7 | async-start | bytes 5013504 | tf_op jit(solution)/shard_map/reduce_scatter | solution.py:80
  342.1 324.8 %reduce-scatter.3.cloned.1.call-start = ((), (), s32[]{:S(2)}) async-start(), calls=%async_computation.5 | async-start | bytes 8912896 | tf_op jit(solution)/shard_map/reduce_scatter | solution.py:88
Sparse Core Ops, SparseCore 0:
  10.5 75.0 all-gather.1
  97.9 77.2 all-reduce.5
  253.2 76.7 all-reduce.7
  334.4 139.4 all-reduce.9
  477.9 83.9 reduce-scatter.4
  566.0 100.7 reduce-scatter.2
where the time goes:
time: 677 us; the launch traced here: 676 us
  waiting for transfers between devices  397 us (59%)
  blocking collectives  167 us (25%)
  matrix products  58.3 us (9%)
  other arithmetic  34.4 us (5%)
  between operations  14.2 us (2%)
    reduce_scatter x1, waiting for transfers between devices, on_device(): lax.psum_scatter(inner(tokens, dpre).astype(jnp.bfloat16), 'row', scatter...  103 us
    reduce_scatter x1, waiting for transfers between devices, on_device(): lax.psum_scatter(inner(student_n, grad_s).astype(jnp.bfloat16), 'row', sc...  85.6 us
    psum x1, waiting for transfers between devices, on_device(): dnorm = lax.psum(dnorm_part, 'proto')  76.8 us
    psum x1, blocking collectives, on_device(): loss = lax.psum(jnp.sum(weight * cross), ('row', 'proto'))  63.4 us
    psum x1, waiting for transfers between devices, on_device(): lax.psum(inner(hidden, dbott).astype(jnp.bfloat16), 'row')  57.5 us
    psum x1, blocking collectives, on_device(): counts = lax.psum(jnp.sum(onehot, axis=0), 'row')  38.4 us
    psum x1, waiting for transfers between devices, on_device(): bott = lax.psum(partial_value, 'proto')  37 us
    all_gather x1, waiting for transfers between devices, on_device(): lax.all_gather(w_in, 'row', axis=0, tiled=True)  35.8 us
  transfers between devices with their start and end apart: 6, of which 6 were waited for; matrix products, arithmetic and copies ran while one was open for 5% of the time, Pallas kernels for 0%

commit v1 on v0

--- a/solution.py
+++ b/solution.py
@@ -52,7 +52,11 @@
     counts = lax.psum(jnp.sum(onehot, axis=0), "row")
     weight = 1.0 / (images * jnp.sum(onehot * counts[None, :], axis=1))
     pre = jnp.dot(
-        tokens, lax.all_gather(w_in, "row", axis=0, tiled=True), preferred_element_type=jnp.float32
+        tokens,
+        jnp.concatenate(
+            lax.all_to_all(jnp.stack([w_in] * lax.axis_size("row")), "row", 0, 0), axis=0
+        ),
+        preferred_element_type=jnp.float32,
     )
     act, slope = gelu_parts(pre)
     hidden = act.astype(jnp.bfloat16)

time: 677 us -> 764 us (1.13)
  blocking collectives: 167 us -> 282 us
  waiting for transfers between devices: 397 us -> 360 us
    psum x1, blocking collectives: 38.4 us -> 154 us  [on_device(): counts = lax.psum(jnp.sum(onehot, axis=0), 'row')]
    all_gather x1 -> x0, waiting for transfers between devices: 35.8 us -> none  [on_device(): lax.all_gather(w_in, 'row', axis=0, tiled=True)]
  transfers between devices with their start and end apart: 6 -> 6, of which waited for: 6 -> 5; matrix products, arithmetic and copies ran while one was open for 5% -> 4% of each run, Pallas kernels for 0% -> 0%
where the time goes in v1:
time: 764 us
  waiting for transfers between devices  360 us (47%)
  blocking collectives  282 us (37%)
  matrix products  58.3 us (8%)
  other arithmetic  31.5 us (4%)
  between operations  13.9 us (2%)
  local copies, waits for them, and re-layouts  10.3 us (1%)
    psum x1, blocking collectives, on_device(): counts = lax.psum(jnp.sum(onehot, axis=0), 'row')  154 us
    reduce_scatter x1, waiting for transfers between devices, on_device(): lax.psum_scatter(inner(tokens, dpre).astype(jnp.bfloat16), 'row', scatter...  103 us
    reduce_scatter x1, waiting for transfers between devices, on_device(): lax.psum_scatter(inner(student_n, grad_s).astype(jnp.bfloat16), 'row', sc...  85.6 us
    psum x1, waiting for transfers between devices, on_device(): dnorm = lax.psum(dnorm_part, 'proto')  76.8 us
    psum x1, blocking collectives, on_device(): loss = lax.psum(jnp.sum(weight * cross), ('row', 'proto'))  63.4 us
    psum x1, waiting for transfers between devices, on_device(): lax.psum(inner(hidden, dbott).astype(jnp.bfloat16), 'row')  57.5 us
    psum x1, waiting for transfers between devices, on_device(): bott = lax.psum(partial_value, 'proto')  36.8 us
    all_gather x1, blocking collectives, on_device(): lax.all_gather(teacher_norm(teacher_z), 'proto', axis=0, tiled=True)  31.2 us
  transfers between devices with their start and end apart: 6, of which 5 were waited for; matrix products, arithmetic and copies ran while one was open for 4% of the time, Pallas kernels for 0%

profile of v1, /device:TPU:0, one launch (start us, length us, event | category | flops | bytes accessed | tf_op | source)
XLA Modules:
  0.0 763.8 jit_solution(906880747237233244)
XLA Ops:
  7.2 5.4 stack.2
  12.6 7.3 all-to-all-start
  20.1 153.6 %psum.49 = f32[64]{0:T(128)S(1)} all-reduce(f32[64]{0:T(128)S(1)} %convert_reduce_fusion), channel_id=1, replica_groups=mesh['row'=16,'proto'=8] {'row'}, use_global_device_ids=true, to_apply=%region_1.0 | all-reduce | flops 64 | bytes 512 | tf_op jit(solution)/shard_map/psum | solution.py:52
  174.0 10.6 %multiply_convert_fusion.1 = (bf16[512,1024]{1,0:T(8,128)(2,1)S(1)}, f32[512,1024]{1,0:T(8,128)}) fusion(bf16[512,4096]{1,0:T(8,128)(2,1)} %param.8, bf16[4096,1024]{1,0:T(8,128)(2,1)} %bitcast), kind=kOutput, calls=%fused_computation.19 | convolution fusion | flops 4297588736 | bytes 15728640 | tf_op jit(solution)/shard_map/dot_general | solution.py:54
  186.3 31.2 %all_gather.3 = bf16[512,384]{1,0:T(8,128)(2,1)S(1)} all-gather(bf16[64,384]{1,0:T(8,128)(2,1)S(1)} %fusion.10), channel_id=1, replica_groups=mesh['row'=16,'proto'=8] {'proto'}, dimensions={0}, use_global_device_ids=true | all-gather | bytes 442368 | tf_op jit(solution)/shard_map/all_gather | solution.py:67
  217.5 9.0 %fusion = (f32[512]{0:T(512)S(1)}, f32[512,6144]{1,0:T(8,128)}) fusion(f32[6144]{0:T(1024)S(1)} %copy-done.4, bf16[512,384]{1,0:T(8,128)(2,1)S(1)} %all_gather.3, bf16[384,6144]{1,0:T(8,128)(2,1)} %param.13), kind=kOutput, calls=%fused_computation.7 | convolution fusion | flops 2425355776 | bytes 17721344 | tf_op jit(solution)/shard_map/dot_general | solution.py:69
  226.5 36.8 %all-reduce.6.cloned.1.call-done = f32[512,384]{1,0:T(8,128)} async-done(((f32[512,384]{1,0:T(8,128)}), f32[512,384]{1,0:T(8,128)}) %all-reduce.6.cloned.1.call-update) | async-done | bytes 786448 | tf_op jit(solution)/shard_map/psum | solution.py:64
  264.6 10.6 %multiply_reduce_fusion.1 = (f32[512]{0:T(512)S(1)}, f32[512,6144]{1,0:T(8,128)}) fusion(bf16[384,6144]{1,0:T(8,128)(2,1)} %param.12, f32[512,384]{1,0:T(8,128)} %all-reduce.6.cloned.1.call-done, f32[512]{0:T(512)S(1)} %add_rsqrt_fusion), kind=kOutput, calls=%fused_computation.6 | convolution fusion | flops 2422603264 | bytes 18092032 | tf_op jit(solution)/shard_map/dot_general | solution.py:71
  275.3 17.9 %all-reduce.1 = (f32[512]{0:T(512)S(1)}, f32[512]{0:T(512)S(1)}) all-reduce(f32[512]{0:T(512)S(1)} %get-tuple-element.20, f32[512]{0:T(512)S(1)} %get-tuple-element.22), channel_id=1, replica_groups=mesh['row'=16,'proto'=8] {'proto'}, use_global_device_ids=true, to_apply=%region_11.0 | all-reduce | flops 1024 | bytes 8192 | tf_op jit(solution)/shard_map/pmax | solution.py:74
  293.1 10.3 %exponential_reduce_fusion = (f32[512]{0:T(512)S(1)}, f32[512]{0:T(512)S(1)}) fusion(f32[512,6144]{1,0:T(8,128)} %get-tuple-element.21, f32[512]{0:T(512)S(1)} %get-tuple-element.14, f32[512]{0:T(512)S(1)} %get-tuple-element.15, f32[512,6144]{1,0:T(8,128)} %get-tuple-element.23, f32[6144]{0:T(1024)S(1)} %copy-done.4), kind=kLoop, calls=%fused_computation.4 | loop fusion | flops 22019072 | bytes 25198592 | tf_op jit(solution)/shard_map/reduce_sum | solution.py:77
  303.4 16.4 %all-reduce = (f32[512]{0:T(512)S(1)}, f32[512]{0:T(512)S(1)}) all-reduce(f32[512]{0:T(512)S(1)} %get-tuple-element.24, f32[512]{0:T(512)S(1)} %get-tuple-element.25), channel_id=1, replica_groups=mesh['row'=16,'proto'=8] {'proto'}, use_global_device_ids=true, to_apply=%region_13.0 | all-reduce | flops 1024 | bytes 8192 | tf_op jit(solution)/shard_map/psum | solution.py:77
  319.8 12.0 %multiply_convert_fusion = (bf16[512,6144]{1,0:T(8,128)(2,1)S(1)}, f32[512]{0:T(512)S(1)}) fusion(f32[512,6144]{1,0:T(8,128)} %get-tuple-element.21, f32[512]{0:T(512)S(1)} %get-tuple-element.12, f32[512]{0:T(512)S(1)} %broadcast_multiply_fusion, f32[512]{0:T(512)S(1)} %get-tuple-element.14, f32[512]{0:T(512)S(1)} %get-tuple-element.13, ...), kind=kLoop, calls=%fused_computation | loop fusion | flops 44039680 | bytes 31496192 | tf_op jit(solution)/shard_map/convert_element_type | solution.py:83
  331.8 2.7 copy-done.1
  334.4 6.7 fusion.15
  341.2 76.8 %all-reduce.8.cloned.1.call-done = f32[512,384]{1,0:T(8,128)} async-done(((f32[512,384]{1,0:T(8,128)}), f32[512,384]{1,0:T(8,128)}) %all-reduce.8.cloned.1.call-update) | async-done | bytes 786448 | tf_op jit(solution)/shard_map/psum | solution.py:88
  422.5 7.7 %convolution_convert_fusion = bf16[384,6144]{1,0:T(8,128)(2,1)} fusion(bf16[512,6144]{1,0:T(8,128)(2,1)} %copy-done.1, f32[512,384]{1,0:T(8,128)S(1)} %copy-done.2, f32[512]{0:T(512)S(1)} %add_rsqrt_fusion), kind=kOutput, calls=%fused_computation.10 | convolution fusion | flops 2418671616 | bytes 11798528 | tf_op jit(solution)/shard_map/dot_general | solution.py:19
  430.2 10.4 %convert_bitcast_fusion = bf16[4096,1024]{0,1:T(8,128)(2,1)} fusion(bf16[512,4096]{1,0:T(8,128)(2,1)} %param.8, f32[512,1024]{1,0:T(8,128)} %get-tuple-element.19, bf16[512,384]{1,0:T(8,128)(2,1)S(1)} %multiply_convert_fusion.2, bf16[1024,384]{1,0:T(8,128)(2,1)S(1)} %copy-done), kind=kOutput, calls=%fused_computation.11 | convolution fusion | flops 4707057664 | bytes 15859712 | tf_op jit(solution)/shard_map/dot_general | solution.py:19
  441.2 63.4 %psum.53 = f32[]{:T(128)} all-reduce(f32[]{:T(128)} %multiply_reduce_fusion.4), channel_id=1, replica_groups=mesh['row'=16,'proto'=8] {'row','proto'}, use_global_device_ids=true, to_apply=%region_16.0 | all-reduce | flops 1 | bytes 8 | tf_op jit(solution)/shard_map/psum | solution.py:82
  504.6 57.5 %all-reduce.10.cloned.1.call-done = bf16[1024,384]{1,0:T(8,128)(2,1)} async-done(((bf16[1024,384]{1,0:T(8,128)(2,1)}), bf16[1024,384]{1,0:T(8,128)(2,1)}) %all-reduce.10.cloned.1.call-update) | async-done | bytes 786448 | tf_op jit(solution)/shard_map/psum | solution.py:90
  562.1 2.4 convert_element_type.57
  564.5 85.6 %reduce-scatter.5.cloned.1.call-done = bf16[24,6144]{1,0:T(8,128)(2,1)} async-done(((bf16[384,6144]{1,0:T(8,128)(2,1)}), bf16[24,6144]{1,0:T(8,128)(2,1)}) %reduce-scatter.5.cloned.1.call-update) | async-done | bytes 294928 | tf_op jit(solution)/shard_map/reduce_scatter | solution.py:84
  650.1 1.8 convert_element_type.59
  651.9 103.1 %reduce-scatter.3.cloned.1.call-done = bf16[256,1024]{0,1:T(8,128)(2,1)} async-done(((bf16[4096,1024]{0,1:T(8,128)(2,1)}), bf16[256,1024]{0,1:T(8,128)(2,1)}) %reduce-scatter.3.cloned.1.call-update) | async-done | bytes 524304 | tf_op jit(solution)/shard_map/reduce_scatter | solution.py:92
  755.0 2.2 copy.13
  (36 shorter events, 8.6 us)
Async XLA Ops:
  7.2 177.5 %copy-start = (bf16[1024,384]{1,0:T(8,128)(2,1)S(1)}, bf16[1024,384]{1,0:T(8,128)(2,1)}, u32[]{:S(2)}) copy-start(bf16[1024,384]{1,0:T(8,128)(2,1)} %param.10) | copy-start | bytes 2359300
  12.6 7.4 copy-start.5
  12.6 161.1 %copy-start.3 = (bf16[64,384]{1,0:T(8,128)(2,1)S(1)}, bf16[64,384]{1,0:T(8,128)(2,1)}, u32[]{:S(2)}) copy-start(bf16[64,384]{1,0:T(8,128)(2,1)} %param.11) | copy-start | bytes 147460
  12.6 161.4 %all-to-all-start = ((bf16[16,256,1024]{2,1,0:T(8,128)(2,1)}), bf16[16,256,1024]{2,1,0:T(8,128)(2,1)}, u32[]{:S(2)}, u32[]{:S(2)}) async-start(bf16[16,256,1024]{2,1,0:T(8,128)(2,1)} %stack.2), calls=%async_computation | async-start | bytes 16777216 | tf_op jit(solution)/shard_map/all_to_all | solution.py:57
  19.9 243.4 %all-reduce.6.cloned.1.call-start = ((), (), s32[]{:S(2)}) async-start(), calls=%async_computation.3 | async-start | bytes 1572864 | tf_op jit(solution)/shard_map/psum | solution.py:64
  174.0 43.5 %copy-start.4 = (f32[6144]{0:T(1024)S(1)}, f32[6144]{0:T(1024)}, u32[]{:S(2)}) copy-start(f32[6144]{0:T(1024)} %param.14) | copy-start | bytes 73732
  186.2 231.8 %all-reduce.8.cloned.1.call-start = ((), (), s32[]{:S(2)}) async-start(), calls=%async_computation.4 | async-start | bytes 1572864 | tf_op jit(solution)/shard_map/psum | solution.py:88
  331.8 2.7 copy-start.1
  334.4 83.6 %copy-start.2 = (f32[512,384]{1,0:T(8,128)S(1)}, f32[512,384]{1,0:T(8,128)}, u32[]{:S(2)}) copy-start(f32[512,384]{1,0:T(8,128)} %all-reduce.6.cloned.1.call-done) | copy-start | bytes 2359300
  341.2 220.9 %all-reduce.10.cloned.1.call-start = ((), (), s32[]{:S(2)}) async-start(), calls=%async_computation.6 | async-start | bytes 1572864 | tf_op jit(solution)/shard_map/psum | solution.py:90
  422.4 227.6 %reduce-scatter.5.cloned.1.call-start = ((), (), s32[]{:S(2)}) async-start(), calls=%async_computation.7 | async-start | bytes 5013504 | tf_op jit(solution)/shard_map/reduce_scatter | solution.py:84
  430.2 324.8 %reduce-scatter.3.cloned.1.call-start = ((), (), s32[]{:S(2)}) async-start(), calls=%async_computation.5 | async-start | bytes 8912896 | tf_op jit(solution)/shard_map/reduce_scatter | solution.py:92
Sparse Core Ops, SparseCore 0:
  186.4 76.8 all-reduce.5
  341.3 76.7 all-reduce.7
  422.6 139.4 all-reduce.9
  566.1 83.9 reduce-scatter.4
  654.2 100.7 reduce-scatter.2
